TPU v7x, 32 devices: a whole 2x2x4 slice. The times are simulated.
32 devices in a mesh: pat: 8 (over y, x, core), src: 4 (over z).
Axes of the slice: x: 2, y: 2, z: 4, core: 2. Of those that a mesh axis runs over, the one named last changes fastest.
Arguments:
- patterns: bfloat16 [8192, 12288], P('src', 'pat'), may hold values from -6 to 6
- left_factors: bfloat16 [3, 8, 512, 1024], P(None, 'src', 'pat'), may hold values from -0.125 to 0.125
- right_factors: bfloat16 [3, 8, 512, 1024], P(None, 'src', 'pat'), may hold values from -0.1875 to 0.1875
- ranks: int32 [3, 8], replicated, may hold values from 128 to 512, as said below
- source_slot_tile: int32 [8], replicated, may hold values from 0 to 7, each once
Outputs:
- potentials: float32 [3072, 12288], P('src', 'pat')
Inputs may be any that keep to these rules, and one draw needn't show every extreme that they name: `ranks`: some tile has rank exactly 512 and some exactly 128. `source_slot_tile`: every source tile is held by exactly one slot.
All inputs are finite; a program needn't handle non-finite values.
Results may differ from a plain program's by a relative error of at most 0.01.
Values may be sent and summed in bfloat16 or wider, within the bound.
No kernel may reach another device: no remote copies, remote signals or barrier semaphores. Data moves between devices by JAX's collectives and lax.ppermute only.
A program may use at most 576 MiB of HBM per device.

v0:
```python
import jax
import jax.numpy as jnp
from jax import lax
from jax.sharding import PartitionSpec as P


def body(patterns, left_factors, right_factors, ranks, source_slot_tile):
    trows, slots, rank_cols, tile = left_factors.shape
    rank_width = patterns.shape[1]
    slab_pieces = patterns.reshape(slots, tile, rank_width)
    total_slots = source_slot_tile.shape[0]
    slot_here = lax.axis_index("src") * slots + jnp.arange(slots, dtype=jnp.int32)
    catalog = jnp.arange(total_slots, dtype=jnp.int32)
    pick_slot = (catalog[None, :] == slot_here[:, None]).astype(jnp.int32)
    tile_here = jnp.sum(pick_slot * source_slot_tile[None, :], axis=1)
    pick_tile = (catalog[None, :] == tile_here[:, None]).astype(jnp.int32)
    rank_here = jnp.sum(ranks[:, None, :] * pick_tile[None, :, :], axis=2)
    piece = lax.all_gather(right_factors, "pat", axis=2, tiled=True)
    count = piece.shape[2]
    rows = jnp.arange(count, dtype=jnp.int32)
    coef = jnp.einsum("tsrb,sbp->tsrp", piece, slab_pieces, preferred_element_type=jnp.float32)
    live = rows[None, None, :] < rank_here[:, :, None]
    coef = jnp.where(live[..., None], coef, 0.0).astype(jnp.bfloat16)
    piece = lax.all_gather(left_factors, "pat", axis=2, tiled=True)
    total = jnp.einsum("tsrb,tsrp->tbp", piece, coef, preferred_element_type=jnp.float32)
    partial_value = total.reshape(trows * tile, rank_width)
    return lax.psum_scatter(
        partial_value.astype(jnp.bfloat16), "src", scatter_dimension=0, tiled=True
    ).astype(jnp.float32)


def solution(mesh):
    in_specs = (P("src", "pat"), P(None, "src", "pat", None), P(None, "src", "pat", None), P(), P())
    out_specs = P("src", "pat")
    return jax.shard_map(body, mesh=mesh, in_specs=in_specs, out_specs=out_specs, check_vma=False)
```

profile of v0, /device:TPU:0, one launch (start us, length us, event | category | flops | bytes accessed | tf_op | source)
XLA Modules:
  0.0 303.1 jit_solution(10433320378242377923)
XLA Ops:
  6.5 0.0 all-gather.5.cloned.1.call-start
  6.5 0.7 all-gather.5.cloned.1.call-update
  7.3 0.0 all-gather.3.cloned.1.call-start
  7.3 0.7 all-gather.3.cloned.1.call-update
  8.0 0.0 reduce-scatter.2.cloned.1.call-start
  8.1 0.8 fusion.9
  8.9 0.1 compare_convert_fusion
  9.0 0.8 multiply_reduce_fusion
  9.8 0.1 iota_compare_fusion
  9.9 47.5 %all-gather.5.cloned.1.call-done = bf16[3,2,512,1024]{3,2,1,0:T(8,128)(2,1)} async-done(((bf16[3,2,64,1024]{3,2,1,0:T(8,128)(2,1)}), bf16[3,2,512,1024]{3,2,1,0:T(8,128)(2,1)}) %all-gather.5.cloned.1.call-update) | async-done | bytes 6291472 | tf_op jit(solution)/shard_map/all_gather | solution.py:24
  57.4 47.3 %all-gather.3.cloned.1.call-done = bf16[3,2,512,1024]{3,2,1,0:T(8,128)(2,1)} async-done(((bf16[3,2,64,1024]{3,2,1,0:T(8,128)(2,1)}), bf16[3,2,512,1024]{3,2,1,0:T(8,128)(2,1)}) %all-gather.3.cloned.1.call-update) | async-done | bytes 6291472 | tf_op jit(solution)/shard_map/all_gather | solution.py:18
  104.7 26.0 %bitcast_convert_fusion = bf16[3,1536,1024]{1,2,0:T(8,128)(2,1)} fusion(bf16[3,2,512,1024]{3,2,1,0:T(8,128)(2,1)} %all-gather.5.cloned.1.call-done, pred[3,2,512]{2,1,0:T(4,128)(4,1)S(1)} %iota_compare_fusion, bf16[2,1024,1536,1]{2,1,0,3:T(8,128)(2,1)} %bitcast.20, bf16[3,2,512,1024]{3,2,1,0:T(8,128)(2,1)} %all-gather.3.cloned.1.call-done), kind=kOutput, calls=%fused_computation | convolution fusion | flops 19341508608 | bytes 28314624 | tf_op jit(solution)/shard_map/tsrb,tsrp->tbp/dot_general | solution.py:25
  130.7 0.0 reduce-scatter.2.cloned.1.call-update
  130.8 161.3 %reduce-scatter.2.cloned.1.call-done = bf16[768,1536]{1,0:T(8,128)(2,1)} async-done(((bf16[3072,1536]{1,0:T(8,128)(2,1)}), bf16[768,1536]{1,0:T(8,128)(2,1)}) %reduce-scatter.2.cloned.1.call-update) | async-done | bytes 2359312 | tf_op jit(solution)/shard_map/reduce_scatter | solution.py:27
  292.1 4.5 %convert_element_type.28 = f32[768,1536]{1,0:T(8,128)} convert(bf16[768,1536]{1,0:T(8,128)(2,1)} %reduce-scatter.2.cloned.1.call-done) | non-fusion elementwise | flops 1179648 | bytes 7077888 | tf_op jit(solution)/shard_map/convert_element_type | solution.py:29
  (1 shorter events, 0.0 us)
Async XLA Ops:
  6.5 50.8 %all-gather.5.cloned.1.call-start = ((), (), s32[]{:S(2)}) async-start(), calls=%async_computation.2 | async-start | bytes 7077888 | tf_op jit(solution)/shard_map/all_gather | solution.py:24
  7.3 97.5 %all-gather.3.cloned.1.call-start = ((), (), s32[]{:S(2)}) async-start(), calls=%async_computation.1 | async-start | bytes 7077888 | tf_op jit(solution)/shard_map/all_gather | solution.py:18
  8.0 284.1 %reduce-scatter.2.cloned.1.call-start = ((), (), s32[]{:S(2)}) async-start(), calls=%async_computation.3 | async-start | bytes 11796480 | tf_op jit(solution)/shard_map/reduce_scatter | solution.py:27
Sparse Core Ops, SparseCore 0:
  9.2 48.1 all-gather.4
  59.3 45.3 all-gather.2
  130.9 161.1 reduce-scatter.1
where the time goes:
time: 303 us
  waiting for transfers between devices  258 us (85%)
  matrix products  26 us (9%)
  between operations  13.1 us (4%)
  other arithmetic  6.32 us (2%)
    reduce_scatter x1, waiting for transfers between devices, body(): lax.psum_scatter(partial_value.astype(jnp.bfloat16), 'src', scatter_dimen...  161 us
    all_gather x1, waiting for transfers between devices, body(): piece = lax.all_gather(left_factors, 'pat', axis=2, tiled=True)  47.5 us
    all_gather x1, waiting for transfers between devices, body(): piece = lax.all_gather(right_factors, 'pat', axis=2, tiled=True)  47.3 us
    dot_general x1, matrix products, body(): jnp.einsum('tsrb,tsrp->tbp', piece, coef, preferred_element_type=jnp.floa...  26 us
  transfers between devices with their start and end apart: 3, of which 3 were waited for; matrix products, arithmetic and copies ran while one was open for 1% of the time, Pallas kernels for 0%

commit v1 on v0

--- a/solution.py
+++ b/solution.py
@@ -2,6 +2,17 @@
 import jax.numpy as jnp
 from jax import lax
 from jax.sharding import PartitionSpec as P
+
+
+def collect(x, axis, dim):
+    ways = lax.axis_size(axis)
+    pieces = [x]
+    for far in range(1, ways):
+        pieces.append(
+            lax.ppermute(pieces[far - 1], axis, [(d, (d - 1) % ways) for d in range(ways)])
+        )
+    line = jnp.concatenate(pieces, axis=dim)
+    return jnp.roll(line, lax.axis_index(axis) * x.shape[dim], axis=dim)
 
 
 def body(patterns, left_factors, right_factors, ranks, source_slot_tile):
@@ -21,7 +32,7 @@
     coef = jnp.einsum("tsrb,sbp->tsrp", piece, slab_pieces, preferred_element_type=jnp.float32)
     live = rows[None, None, :] < rank_here[:, :, None]
     coef = jnp.where(live[..., None], coef, 0.0).astype(jnp.bfloat16)
-    piece = lax.all_gather(left_factors, "pat", axis=2, tiled=True)
+    piece = collect(left_factors, "pat", 2)
     total = jnp.einsum("tsrb,tsrp->tbp", piece, coef, preferred_element_type=jnp.float32)
     partial_value = total.reshape(trows * tile, rank_width)
     return lax.psum_scatter(

time: 303 us -> 354 us (1.17)
  local copies, waits for them, and re-layouts: 0 us -> 50.1 us
  waiting for transfers between devices: 258 us -> 233 us
  starting transfers between devices: 0.08 us -> 20.5 us
    ppermute x0 -> x7, waiting for transfers between devices: none -> 71.3 us  [collect(): lax.ppermute(pieces[far - 1], axis, [(d, (d - 1) % ways) for d in range(w...]
    all_gather x1 -> x0, waiting for transfers between devices: 47.5 us -> none  [body(): piece = lax.all_gather(left_factors, 'pat', axis=2, tiled=True)]
    all_gather x1, waiting for transfers between devices: 47.3 us -> 0.02 us  [body(): piece = lax.all_gather(right_factors, 'pat', axis=2, tiled=True)]
    concatenate x0 -> x1, local copies, waits for them, and re-layouts: none -> 28.1 us  [collect(): return jnp.roll(line, lax.axis_index(axis) * x.shape[dim], axis=dim)]
    ppermute x0 -> x7, starting transfers between devices: none -> 20.4 us  [collect(): lax.ppermute(pieces[far - 1], axis, [(d, (d - 1) % ways) for d in range(w...]
    ppermute x0 -> x7, local copies, waits for them, and re-layouts: none -> 16.6 us  [collect(): lax.ppermute(pieces[far - 1], axis, [(d, (d - 1) % ways) for d in range(w...]
    unnamed x0 -> x11, local copies, waits for them, and re-layouts: none -> 5.37 us
  transfers between devices with their start and end apart: 3 -> 9, of which waited for: 3 -> 7; matrix products, arithmetic and copies ran while one was open for 1% -> 14% of each run, Pallas kernels for 0% -> 0%
where the time goes in v1:
time: 354 us; the launch traced here: 351 us
  waiting for transfers between devices  233 us (66%)
  local copies, waits for them, and re-layouts  50.1 us (14%)
  matrix products  27.4 us (8%)
  starting transfers between devices  20.5 us (6%)
  between operations  13.5 us (4%)
  other arithmetic  6.31 us (2%)
    reduce_scatter x1, waiting for transfers between devices, body(): lax.psum_scatter(partial_value.astype(jnp.bfloat16), 'src', scatter_dimen...  161 us
    ppermute x7, waiting for transfers between devices, collect(): lax.ppermute(pieces[far - 1], axis, [(d, (d - 1) % ways) for d in range(w...  71.3 us
    concatenate x1, local copies, waits for them, and re-layouts, collect(): return jnp.roll(line, lax.axis_index(axis) * x.shape[dim], axis=dim)  28.1 us
    dot_general x1, matrix products, body(): jnp.einsum('tsrb,tsrp->tbp', piece, coef, preferred_element_type=jnp.floa...  27.4 us
    ppermute x7, starting transfers between devices, collect(): lax.ppermute(pieces[far - 1], axis, [(d, (d - 1) % ways) for d in range(w...  20.4 us
    ppermute x7, local copies, waits for them, and re-layouts, collect(): lax.ppermute(pieces[far - 1], axis, [(d, (d - 1) % ways) for d in range(w...  16.6 us
  transfers between devices with their start and end apart: 9, of which 7 were waited for; matrix products, arithmetic and copies ran while one was open for 14% of the time, Pallas kernels for 0%

profile of v1, /device:TPU:0, one launch (start us, length us, event | category | flops | bytes accessed | tf_op | source)
XLA Modules:
  0.0 351.1 jit_solution(11420012886367738226)
XLA Ops:
  6.5 0.0 all-gather.2.cloned.1.call-start
  6.5 0.7 all-gather.2.cloned.1.call-update
  7.3 0.0 reduce-scatter.2.cloned.1.call-start
  7.3 3.4 collective-permute-start
  10.7 10.4 %collective-permute-done = bf16[3,2,64,1024]{3,2,1,0:T(8,128)(2,1)S(1)} collective-permute-done((bf16[3,2,64,1024]{3,2,1,0:T(8,128)(2,1)}, bf16[3,2,64,1024]{3,2,1,0:T(8,128)(2,1)S(1)}, u32[]{:S(2)}, u32[]{:S(2)}) %collective-permute-start) | collective-permute-done | bytes 786464 | tf_op jit(solution)/shard_map/ppermute | solution.py:12
  21.1 0.0 copy-start
  21.1 0.9 copy-done
  22.0 2.7 collective-permute-start.1
  24.7 12.6 %collective-permute-done.1 = bf16[3,2,64,1024]{3,2,1,0:T(8,128)(2,1)S(1)} collective-permute-done((bf16[3,2,64,1024]{3,2,1,0:T(8,128)(2,1)S(1)}, bf16[3,2,64,1024]{3,2,1,0:T(8,128)(2,1)S(1)}, u32[]{:S(2)}, u32[]{:S(2)}) %collective-permute-start.1) | collective-permute-done | bytes 786464 | tf_op jit(solution)/shard_map/ppermute | solution.py:12
  37.3 0.0 copy-start.1
  37.3 0.9 copy-done.1
  38.2 2.9 collective-permute-start.2
  41.1 20.4 %collective-permute-done.2 = bf16[3,2,64,1024]{3,2,1,0:T(8,128)(2,1)S(1)} collective-permute-done((bf16[3,2,64,1024]{3,2,1,0:T(8,128)(2,1)S(1)}, bf16[3,2,64,1024]{3,2,1,0:T(8,128)(2,1)S(1)}, u32[]{:S(2)}, u32[]{:S(2)}) %collective-permute-start.2) | collective-permute-done | bytes 786464 | tf_op jit(solution)/shard_map/ppermute | solution.py:12
  61.5 0.0 copy-start.2
  61.5 0.9 copy-done.2
  62.4 2.9 collective-permute-start.3
  65.3 10.7 %collective-permute-done.3 = bf16[3,2,64,1024]{3,2,1,0:T(8,128)(2,1)S(1)} collective-permute-done((bf16[3,2,64,1024]{3,2,1,0:T(8,128)(2,1)S(1)}, bf16[3,2,64,1024]{3,2,1,0:T(8,128)(2,1)S(1)}, u32[]{:S(2)}, u32[]{:S(2)}) %collective-permute-start.3) | collective-permute-done | bytes 786464 | tf_op jit(solution)/shard_map/ppermute | solution.py:12
  75.9 0.0 copy-start.3
  75.9 0.9 copy-done.3
  76.8 2.9 collective-permute-start.4
  79.7 9.5 %collective-permute-done.4 = bf16[3,2,64,1024]{3,2,1,0:T(8,128)(2,1)S(1)} collective-permute-done((bf16[3,2,64,1024]{3,2,1,0:T(8,128)(2,1)S(1)}, bf16[3,2,64,1024]{3,2,1,0:T(8,128)(2,1)S(1)}, u32[]{:S(2)}, u32[]{:S(2)}) %collective-permute-start.4) | collective-permute-done | bytes 786464 | tf_op jit(solution)/shard_map/ppermute | solution.py:12
  89.2 0.0 copy-start.4
  89.2 2.8 collective-permute-start.5
  92.0 1.8 copy.25
  93.8 7.7 %collective-permute-done.5 = bf16[3,2,64,1024]{3,2,1,0:T(8,128)(2,1)} collective-permute-done((bf16[3,2,64,1024]{3,2,1,0:T(8,128)(2,1)S(1)}, bf16[3,2,64,1024]{3,2,1,0:T(8,128)(2,1)}, u32[]{:S(2)}, u32[]{:S(2)}) %collective-permute-start.5) | collective-permute-done | bytes 786464 | tf_op jit(solution)/shard_map/ppermute | solution.py:12
  101.5 2.9 collective-permute-start.6
  104.4 0.8 fusion.10
  105.3 0.1 compare_convert_fusion
  105.3 0.8 multiply_reduce_fusion
  106.2 0.0 copy-done.4
  106.2 0.1 iota_compare_fusion
  106.3 1.8 copy.26
  108.1 2.5 copy.27
  110.5 2.5 copy.28
  113.0 2.5 copy.29
  115.5 2.5 copy.30
  118.0 2.5 copy.31
  120.4 0.0 collective-permute-done.6
  120.4 2.5 copy.32
  122.9 28.1 %concatenate.6 = bf16[3,2,1024,1024]{2,3,1,0:T(8,128)(2,1)} concatenate(bf16[3,2,64,1024]{2,3,1,0:T(8,128)(2,1)S(1)} %copy.25, bf16[3,2,64,1024]{2,3,1,0:T(8,128)(2,1)S(1)} %copy.26, bf16[3,2,64,1024]{2,3,1,0:T(8,128)(2,1)} %copy.27, bf16[3,2,64,1024]{2,3,1,0:T(8,128)(2,1)} %copy.28, bf16[3,2,64,1024]{2,3,1,0:T(8,128)(2,1)} %copy.29, bf16[3,2,64,1024]{2,3,1,0:T(8,128)(2,1)} %copy.30, ...), dimensions={2} | concatenate | bytes 25165824 | tf_op jit(solution)/shard_map/jit(_roll_dynamic)/concatenate | solution.py:15
  151.0 0.0 all-gather.2.cloned.1.call-done
  151.0 27.4 %bitcast_convert_fusion = bf16[3,1024,1536]{2,1,0:T(8,128)(2,1)} fusion(pred[3,2,512]{2,1,0:T(4,128)(4,1)S(1)} %iota_compare_fusion, bf16[3,2,1024,1024]{2,3,1,0:T(8,128)(2,1)} %concatenate.6, s32[]{:T(128)S(6)} %select_n.18, bf16[2,1024,1536,1]{2,1,0,3:T(8,128)(2,1)} %bitcast.17, bf16[3,2,512,1024]{3,2,1,0:T(8,128)(2,1)} %all-gather.2.cloned.1.call-done), kind=kOutput, calls=%fused_computation | convolution fusion | flops 19341508608 | bytes 28314628 | tf_op jit(solution)/shard_map/tsrb,tsrp->tbp/dot_general | solution.py:36
  178.4 0.0 reduce-scatter.2.cloned.1.call-update
  178.4 161.3 %reduce-scatter.2.cloned.1.call-done = bf16[768,1536]{1,0:T(8,128)(2,1)} async-done(((bf16[3072,1536]{1,0:T(8,128)(2,1)}), bf16[768,1536]{1,0:T(8,128)(2,1)}) %reduce-scatter.2.cloned.1.call-update) | async-done | bytes 2359312 | tf_op jit(solution)/shard_map/reduce_scatter | solution.py:38
  339.7 4.5 %convert_element_type.24 = f32[768,1536]{1,0:T(8,128)} convert(bf16[768,1536]{1,0:T(8,128)(2,1)} %reduce-scatter.2.cloned.1.call-done) | non-fusion elementwise | flops 1179648 | bytes 7077888 | tf_op jit(solution)/shard_map/convert_element_type | solution.py:40
  (1 shorter events, 0.0 us)
Async XLA Ops:
  6.5 144.4 %all-gather.2.cloned.1.call-start = ((), (), s32[]{:S(2)}) async-start(), calls=%async_computation.1 | async-start | bytes 7077888 | tf_op jit(solution)/shard_map/all_gather | solution.py:29
  7.3 332.5 %reduce-scatter.2.cloned.1.call-start = ((), (), s32[]{:S(2)}) async-start(), calls=%async_computation.2 | async-start | bytes 11796480 | tf_op jit(solution)/shard_map/reduce_scatter | solution.py:38
  7.3 13.8 %collective-permute-start = (bf16[3,2,64,1024]{3,2,1,0:T(8,128)(2,1)}, bf16[3,2,64,1024]{3,2,1,0:T(8,128)(2,1)S(1)}, u32[]{:S(2)}, u32[]{:S(2)}) collective-permute-start(bf16[3,2,64,1024]{3,2,1,0:T(8,128)(2,1)} %param.6), channel_id=1, source_target_pairs={{0,28},{4,0},{8,4},{12,8},{16,12},{20,16},{24,20},{28,24},{1,29},{... | collective-permute-start | bytes 2359304 | tf_op jit(solution)/shard_map/ppermute | solution.py:12
  21.1 0.9 copy-start
  22.0 15.3 %collective-permute-start.1 = (bf16[3,2,64,1024]{3,2,1,0:T(8,128)(2,1)S(1)}, bf16[3,2,64,1024]{3,2,1,0:T(8,128)(2,1)S(1)}, u32[]{:S(2)}, u32[]{:S(2)}) collective-permute-start(bf16[3,2,64,1024]{3,2,1,0:T(8,128)(2,1)S(1)} %collective-permute-done), channel_id=1, source_target_pairs={{0,28},{4,0},{8,4},{12,8},{16,12},{20,16},{24,20},{28,24},{1,29},{... | collective-permute-start | bytes 2359304 | tf_op jit(solution)/shard_map/ppermute | solution.py:12
  37.3 0.9 copy-start.1
  38.2 23.3 %collective-permute-start.2 = (bf16[3,2,64,1024]{3,2,1,0:T(8,128)(2,1)S(1)}, bf16[3,2,64,1024]{3,2,1,0:T(8,128)(2,1)S(1)}, u32[]{:S(2)}, u32[]{:S(2)}) collective-permute-start(bf16[3,2,64,1024]{3,2,1,0:T(8,128)(2,1)S(1)} %collective-permute-done.1), channel_id=1, source_target_pairs={{0,28},{4,0},{8,4},{12,8},{16,12},{20,16},{24,20},{28,24},{1,29},{... | collective-permute-start | bytes 2359304 | tf_op jit(solution)/shard_map/ppermute | solution.py:12
  61.5 0.9 copy-start.2
  62.4 13.5 %collective-permute-start.3 = (bf16[3,2,64,1024]{3,2,1,0:T(8,128)(2,1)S(1)}, bf16[3,2,64,1024]{3,2,1,0:T(8,128)(2,1)S(1)}, u32[]{:S(2)}, u32[]{:S(2)}) collective-permute-start(bf16[3,2,64,1024]{3,2,1,0:T(8,128)(2,1)S(1)} %collective-permute-done.2), channel_id=1, source_target_pairs={{0,28},{4,0},{8,4},{12,8},{16,12},{20,16},{24,20},{28,24},{1,29},{... | collective-permute-start | bytes 2359304 | tf_op jit(solution)/shard_map/ppermute | solution.py:12
  75.9 0.9 copy-start.3
  76.8 12.4 %collective-permute-start.4 = (bf16[3,2,64,1024]{3,2,1,0:T(8,128)(2,1)S(1)}, bf16[3,2,64,1024]{3,2,1,0:T(8,128)(2,1)S(1)}, u32[]{:S(2)}, u32[]{:S(2)}) collective-permute-start(bf16[3,2,64,1024]{3,2,1,0:T(8,128)(2,1)S(1)} %collective-permute-done.3), channel_id=1, source_target_pairs={{0,28},{4,0},{8,4},{12,8},{16,12},{20,16},{24,20},{28,24},{1,29},{... | collective-permute-start | bytes 2359304 | tf_op jit(solution)/shard_map/ppermute | solution.py:12
  89.2 17.0 %copy-start.4 = (bf16[3,2,64,1024]{3,2,1,0:T(8,128)(2,1)}, bf16[3,2,64,1024]{3,2,1,0:T(8,128)(2,1)S(1)}, u32[]{:S(2)}) copy-start(bf16[3,2,64,1024]{3,2,1,0:T(8,128)(2,1)S(1)} %collective-permute-done.4) | copy-start | bytes 2359300
  89.2 12.3 %collective-permute-start.5 = (bf16[3,2,64,1024]{3,2,1,0:T(8,128)(2,1)S(1)}, bf16[3,2,64,1024]{3,2,1,0:T(8,128)(2,1)}, u32[]{:S(2)}, u32[]{:S(2)}) collective-permute-start(bf16[3,2,64,1024]{3,2,1,0:T(8,128)(2,1)S(1)} %collective-permute-done.4), channel_id=1, source_target_pairs={{0,28},{4,0},{8,4},{12,8},{16,12},{20,16},{24,20},{28,24},{1,29},{... | collective-permute-start | bytes 2359304 | tf_op jit(solution)/shard_map/ppermute | solution.py:12
  101.5 18.9 %collective-permute-start.6 = (bf16[3,2,64,1024]{3,2,1,0:T(8,128)(2,1)}, bf16[3,2,64,1024]{3,2,1,0:T(8,128)(2,1)}, u32[]{:S(2)}, u32[]{:S(2)}) collective-permute-start(bf16[3,2,64,1024]{3,2,1,0:T(8,128)(2,1)} %collective-permute-done.5), channel_id=1, source_target_pairs={{0,28},{4,0},{8,4},{12,8},{16,12},{20,16},{24,20},{28,24},{1,29},{... | collective-permute-start | bytes 2359304 | tf_op jit(solution)/shard_map/ppermute | solution.py:12
Sparse Core Ops, SparseCore 0:
  9.2 62.7 all-gather.1
  178.5 161.1 reduce-scatter.1
